TPU v7x, 128 devices: a whole 4x4x4 slice. The times are simulated.
128 devices in a mesh: gx: 8 (over z_lo, x), gy: 4 (over z_hi, core), gz: 4 (over y).
Axes of the slice: x: 4, y: 4, z: 4 (z_hi: 2, z_lo: 2; z = z_hi * 2 + z_lo), core: 2. Of those that a mesh axis runs over, the one named last changes fastest.
Arguments:
- x_saved: bfloat16 [1024, 16384], P('gx', ('gy', 'gz')), may hold values from -0.1875 to 0.1875
- grad_out: bfloat16 [1024, 28672], P('gx', ('gz', 'gy')), may hold values from -6 to 6
- weight: bfloat16 [16384, 28672], P('gy', ('gz', 'gx')), may hold values from -0.09375 to 0.09375
Outputs:
- grad_in: bfloat16 [1024, 16384], P('gx', ('gy', 'gz'))
- grad_weight: bfloat16 [16384, 28672], P('gy', ('gz', 'gx'))
All inputs are finite; a program needn't handle non-finite values.
Results may differ from a plain program's by a relative error of at most 0.001.
Values may be sent and summed in bfloat16 or wider, within the bound.
A program may use at most 128 MiB of HBM per device.

v0:
```python
import jax
import jax.numpy as jnp
from jax import lax
from jax.sharding import PartitionSpec as P


def body(x_saved, grad_out, weight):
    token_rows = x_saved.shape[0]
    token_groups = lax.axis_size("gx")
    feature_groups = lax.axis_size("gz")
    grad_block = lax.all_gather(grad_out, "gy", axis=1, tiled=True)
    grad_all = lax.all_to_all(grad_block, "gx", split_axis=1, concat_axis=0, tiled=True)
    unit_cols = grad_all.shape[1]
    inputs_block = lax.all_gather(x_saved, "gz", axis=1, tiled=True)
    summed = jnp.einsum(
        "td,tc->dc",
        lax.all_gather(inputs_block, "gx", axis=0, tiled=True),
        grad_all,
        preferred_element_type=jnp.float32,
    )
    grad_weight = summed.astype(jnp.bfloat16)
    grad_split = grad_all.reshape(token_groups, token_rows, unit_cols)
    weight_split = weight.reshape(feature_groups, weight.shape[0] // feature_groups, unit_cols)
    terms = jnp.einsum(
        "atc,bkc->abtk", grad_split, weight_split, preferred_element_type=jnp.float32
    )
    terms = terms.reshape(token_groups * feature_groups * token_rows, weight_split.shape[1])
    grad_in = lax.psum_scatter(terms, ("gx", "gz"), scatter_dimension=0, tiled=True)
    return (grad_in.astype(jnp.bfloat16), grad_weight)


def solution(mesh):
    return jax.shard_map(
        body,
        mesh=mesh,
        in_specs=(P("gx", ("gy", "gz")), P("gx", ("gz", "gy")), P("gy", ("gz", "gx"))),
        out_specs=(P("gx", ("gy", "gz")), P("gy", ("gz", "gx"))),
        check_vma=False,
    )
```

profile of v0, /device:TPU:0, one launch (start us, length us, event | category | flops | bytes accessed | tf_op | source)
XLA Modules:
  0.0 386.5 jit_solution(9099532467425328987)
XLA Ops:
  7.2 0.0 all-gather.6.cloned.1.call-start
  7.2 0.7 all-gather.6.cloned.1.call-update
  7.9 0.0 all-gather.4.cloned.1.call-start
  7.9 2.0 copy.5
  9.9 0.0 all-gather.4.cloned.1.call-update
  10.0 0.0 all-gather.8.cloned.1.call-start
  10.0 26.1 %all-gather.6.cloned.1.call-done = bf16[128,4096]{1,0:T(8,128)(2,1)} async-done(((bf16[128,1024]{1,0:T(8,128)(2,1)}), bf16[128,4096]{1,0:T(8,128)(2,1)}) %all-gather.6.cloned.1.call-update) | async-done | bytes 1048592 | tf_op jit(solution)/shard_map/all_gather | solution.py:14
  36.1 0.0 all-gather.8.cloned.1.call-update
  36.2 0.0 reduce-scatter.2.cloned.1.call-start
  36.2 27.8 %all-gather.4.cloned.1.call-done = bf16[128,7168]{0,1:T(8,128)(2,1)} async-done(((bf16[128,1792]{0,1:T(8,128)(2,1)}), bf16[128,7168]{0,1:T(8,128)(2,1)}) %all-gather.4.cloned.1.call-update) | async-done | bytes 1835024 | tf_op jit(solution)/shard_map/all_gather | solution.py:11
  64.0 3.1 copy.6
  67.1 46.1 %all_to_all.19 = bf16[128,8,896]{2,0,1:T(8,128)(2,1)S(1)} all-to-all(bf16[128,8,896]{2,0,1:T(8,128)(2,1)S(1)} %copy.6), channel_id=1, replica_groups=mesh['gx'=8,'gy'=4,'gz'=4] {'gx'}, dimensions={1} | all-to-all | bytes 3670016 | tf_op jit(solution)/shard_map/all_to_all | solution.py:12
  113.2 0.0 copy-start
  113.2 11.8 %convolution_bitcast_fusion = f32[8,4,128,1024]{3,2,0,1:T(8,128)S(1)} fusion(bf16[4,1024,896,1]{2,1,3,0:T(8,128)(2,1)} %bitcast.22, bf16[128,8,896]{2,0,1:T(8,128)(2,1)S(1)} %all_to_all.19), kind=kOutput, calls=%fused_computation | convolution fusion | flops 7516192768 | bytes 25952256 | tf_op jit(solution)/shard_map/atc,bkc->abtk/dot_general | solution.py:24
  125.0 0.0 copy-done
  125.0 6.1 %copy.7 = f32[8,4,128,1024]{3,2,1,0:T(8,128)} copy(f32[8,4,128,1024]{3,2,0,1:T(8,128)S(1)} %convolution_bitcast_fusion) | data formatting | bytes 33554432 | tf_op jit(solution)/shard_map/atc,bkc->abtk/transpose | solution.py:24
  131.1 0.0 copy-start.1
  131.1 0.0 reduce-scatter.2.cloned.1.call-update
  131.1 43.9 %all-gather.8.cloned.1.call-done = bf16[1024,4096]{1,0:T(8,128)(2,1)} async-done(((bf16[128,4096]{1,0:T(8,128)(2,1)}), bf16[1024,4096]{1,0:T(8,128)(2,1)}) %all-gather.8.cloned.1.call-update) | async-done | bytes 8388624 | tf_op jit(solution)/shard_map/all_gather | solution.py:17
  175.0 0.0 copy-done.1
  175.1 14.2 %convolution_convert_fusion = bf16[4096,896]{1,0:T(8,128)(2,1)} fusion(bf16[1024,4096]{1,0:T(8,128)(2,1)} %all-gather.8.cloned.1.call-done, bf16[1024,896]{1,0:T(8,128)(2,1)S(1)} %bitcast.21), kind=kOutput, calls=%fused_computation.1 | convolution fusion | flops 7519862784 | bytes 17563648 | tf_op jit(solution)/shard_map/td,tc->dc/dot_general | solution.py:15
  189.3 189.0 %reduce-scatter.2.cloned.1.call-done = f32[128,1024]{1,0:T(8,128)} async-done(((f32[4096,1024]{1,0:T(8,128)}), f32[128,1024]{1,0:T(8,128)}) %reduce-scatter.2.cloned.1.call-update) | async-done | bytes 524304 | tf_op jit(solution)/shard_map/reduce_scatter | solution.py:28
  378.2 1.8 convert_element_type.6
Async XLA Ops:
  7.2 29.0 %all-gather.6.cloned.1.call-start = ((), (), s32[]{:S(2)}) async-start(), calls=%async_computation.4 | async-start | bytes 1310720 | tf_op jit(solution)/shard_map/all_gather | solution.py:14
  7.9 56.1 %all-gather.4.cloned.1.call-start = ((), (), s32[]{:S(2)}) async-start(), calls=%async_computation.2 | async-start | bytes 2293760 | tf_op jit(solution)/shard_map/all_gather | solution.py:11
  10.0 165.1 %all-gather.8.cloned.1.call-start = ((), (), s32[]{:S(2)}) async-start(), calls=%async_computation.5 | async-start | bytes 9437184 | tf_op jit(solution)/shard_map/all_gather | solution.py:17
  36.2 342.1 %reduce-scatter.2.cloned.1.call-start = ((), (), s32[]{:S(2)}) async-start(), calls=%async_computation.3 | async-start | bytes 17301504 | tf_op jit(solution)/shard_map/reduce_scatter | solution.py:28
  113.2 11.8 %copy-start = (bf16[128,8,896]{2,0,1:T(8,128)(2,1)}, bf16[128,8,896]{2,0,1:T(8,128)(2,1)S(1)}, u32[]{:S(2)}) copy-start(bf16[128,8,896]{2,0,1:T(8,128)(2,1)S(1)} %all_to_all.19) | copy-start | bytes 5505028
  131.1 43.9 %copy-start.1 = (bf16[128,8,896]{2,0,1:T(8,128)(2,1)S(1)}, bf16[128,8,896]{2,0,1:T(8,128)(2,1)}, u32[]{:S(2)}) copy-start(bf16[128,8,896]{2,0,1:T(8,128)(2,1)} %copy-done) | copy-start | bytes 5505028
Sparse Core Ops, SparseCore 0:
  9.7 26.4 all-gather.5
  38.4 25.6 all-gather.3
  65.7 109.3 all-gather.7
  177.3 200.8 reduce-scatter.1
where the time goes:
time: 387 us
  waiting for transfers between devices  288 us (74%)
  blocking collectives  46.1 us (12%)
  matrix products  26 us (7%)
  between operations  13.8 us (4%)
  local copies, waits for them, and re-layouts  11.2 us (3%)
    reduce_scatter x1, waiting for transfers between devices, body(): lax.psum_scatter(terms, ('gx', 'gz'), scatter_dimension=0, tiled=True)  189 us
    all_to_all x1, blocking collectives, body(): lax.all_to_all(grad_block, 'gx', split_axis=1, concat_axis=0, tiled=True)  46.1 us
    all_gather x1, waiting for transfers between devices, body(): lax.all_gather(inputs_block, 'gx', axis=0, tiled=True)  43.9 us
    all_gather x1, waiting for transfers between devices, body(): grad_block = lax.all_gather(grad_out, 'gy', axis=1, tiled=True)  27.8 us
    all_gather x1, waiting for transfers between devices, body(): inputs_block = lax.all_gather(x_saved, 'gz', axis=1, tiled=True)  26.1 us
    dot_general x1, matrix products, body(): jnp.einsum('td,tc->dc', lax.all_gather(inputs_block, 'gx', axis=0, tiled=...  14.2 us
    dot_general x1, matrix products, body(): jnp.einsum('atc,bkc->abtk', grad_split, weight_split, preferred_element_t...  11.8 us
  transfers between devices with their start and end apart: 4, of which 4 were waited for; matrix products, arithmetic and copies ran while one was open for 10% of the time, Pallas kernels for 0%

commit v1 on v0

v1 whole, which is shorter than its diff:
```python
import functools

import jax
import jax.numpy as jnp
from jax import lax
from jax.experimental import pallas as pl
from jax.experimental.pallas import tpu as pltpu
from jax.sharding import PartitionSpec as P

SIZE = {"x": 4, "y": 4, "z": 2}
AXES = ("x", "y", "z")
ROWS = ((0, 256), (256, 384), (640, 384))
GATHER_ORDER = (("x", "y", "z"), ("y", "z", "x"), ("z", "x", "y"))
REDUCE_ORDER = (("y", "x", "z"), ("x", "z", "y"), ("z", "y", "x"))
OFFSETS = tuple((a, b, c) for a in range(4) for b in range(4) for c in range(2))


def index_of(off):
    return (off[0] * 4 + off[1]) * 2 + off[2]


def children(order, off):
    at = dict(zip(AXES, off))
    last = max([i for i in range(3) if at[order[i]]], default=-1)
    found = []

    def child(axis, value):
        moved = dict(at)
        moved[axis] = value
        return tuple(moved[a] for a in AXES)

    if last >= 0 and SIZE[order[last]] == 4:
        axis = order[last]
        if at[axis] == 1:
            found.append((child(axis, 2), axis, 1, 0))
        if at[axis] == 3:
            found.append((child(axis, 2), axis, -1, 1))
    for i in range(last + 1, 3):
        axis = order[i]
        found.append((child(axis, 1), axis, 1, None))
        if SIZE[axis] == 4:
            found.append((child(axis, 3), axis, -1, None))
    return found


def parents(order):
    found = {}
    for off in OFFSETS:
        for kid, axis, step, half in children(order, off):
            found.setdefault(kid, []).append((off, axis, step, half))
    return found


def span(color, half):
    start, rows = ROWS[color]
    if half is None:
        return start, rows
    return start + half * (rows // 2), rows // 2


def plan(wire_bytes, rate=46500.0, delay=1.8, g_time=12.0):
    free = {("x", 1): g_time * 0.8, ("x", -1): g_time * 0.8, ("y", 1): 2.0, ("y", -1): 2.0, ("z", 1): g_time * 0.8}
    arrive = {}

    def send(kind, color, kid, axis, step, half, now, nbytes):
        link = (axis, step if SIZE[axis] == 4 else 1)
        free[link] = max(free[link], now) + nbytes / rate
        arrive[(kind, color, kid, half)] = free[link] + delay

    tasks = {}
    up = [parents(order) for order in REDUCE_ORDER]
    gather_up = [parents(order) for order in GATHER_ORDER]
    for color in range(3):
        for off in OFFSETS:
            tasks[("ag", color, off)] = None
            tasks[("rs", color, off)] = None
    for oy in range(4):
        for color in range(3):
            tasks[("gw", color, oy)] = None
    for ox in range(4):
        for oy in range(4):
            tasks[("pp", ox, oy)] = None
    distance = (0, 1, 2, 1)
    done = {}
    now = 2.0
    program = []

    def ready(task):
        kind, first, off = task
        if kind == "ag":
            if off == (0, 0, 0):
                return 2.0
            need = [("ag", first, off, half) for _, _, _, half in gather_up[first][off]]
            if any(n not in arrive for n in need):
                return None
            return max(arrive[n] for n in need)
        if kind == "rs":
            if ("pp", off[0], off[1]) not in done:
                return None
            need = [("rs", first, kid, half) for kid, _, _, half in children(REDUCE_ORDER[first], off)]
            if any(n not in arrive for n in need):
                return None
            return max([arrive[n] for n in need], default=0.0)
        if kind == "pp":
            return g_time
        if any(("ag", first, (a, off, c)) not in done for a in range(4) for c in range(2)):
            return None
        return g_time

    def rank(task, at):
        kind = task[0]
        if kind in ("ag", "rs"):
            return (0, at, str(task))
        if kind == "pp":
            return (1, -(distance[task[1]] + distance[task[2]]), str(task))
        return (2, 0.0, str(task))

    while tasks:
        options = [(ready(t), t) for t in tasks]
        options = [(r, t) for r, t in options if r is not None]
        open_now = [(r, t) for r, t in options if r <= now]
        if not open_now:
            now = min(r for r, _ in options)
            continue
        _, task = min(open_now, key=lambda item: rank(item[1], item[0]))
        del tasks[task]
        program.append(task)
        kind, first, off = task
        now += {"ag": 0.05, "rs": 0.1, "pp": 0.85, "gw": 1.3}[kind]
        done[task] = now
        if kind == "ag":
            for kid, axis, step, half in children(GATHER_ORDER[first], off):
                send("ag", first, kid, axis, step, half, now, span(first, half)[1] * 256)
        if kind == "rs" and off != (0, 0, 0):
            for _, axis, step, half in up[first][off]:
                send("rs", first, off, axis, -step, half, now, span(first, half)[1] * 128 * wire_bytes)
    return program, now


def body(x_ref, go_ref, w_ref, gi_ref, gw_ref, w_buf, x_all, g_all, part, landed, stage,
         w_sem, ag_send, ag_recv, rs_send, rs_recv, g_send, g_recv, h_send, out_sem, *, program):
    gx, gy, y = lax.axis_index("gx"), lax.axis_index("gy"), lax.axis_index("gz")
    zl, x = gx // 4, gx % 4
    zh, core = gy // 2, gy % 2

    def neighbour(axis, step):
        if axis == "x":
            return {"gx": zl * 4 + (x + step + 4) % 4, "gy": gy, "gz": y}
        if axis == "y":
            return {"gx": gx, "gy": gy, "gz": (y + step + 4) % 4}
        return {"gx": (1 - zl) * 4 + x, "gy": gy, "gz": y}

    def remote(src, dst, send_sem, recv_sem, device):
        return pltpu.make_async_remote_copy(
            src_ref=src, dst_ref=dst, send_sem=send_sem, recv_sem=recv_sem,
            device_id=device, device_id_type=pl.DeviceIdType.MESH)

    w_copy = pltpu.make_async_copy(w_ref, w_buf, w_sem)
    w_copy.start()

    for half in range(2):
        for far in range(2):
            to_x, to_y = zh * 4 + 2 * core + half, far * 2 + zl
            src = go_ref.at[:, pl.ds(half * 896, 896)]
            here = jnp.logical_and(to_x == gx, to_y == gy)

            @pl.when(here)
            def _():
                pltpu.make_async_copy(src, g_all.at[gx], g_recv.at[gx]).start()

            @pl.when(jnp.logical_not(here))
            def _():
                remote(src, g_all.at[gx], g_send.at[2 * half + far], g_recv.at[gx],
                       {"gx": to_x, "gy": to_y, "gz": y}).start()

    own = gx * 4 + y
    x_all[own] = x_ref[...].T

    def gather_slot(off):
        return ((zl + off[2]) % 2 * 4 + (x + 4 - off[0]) % 4) * 4 + (y + 4 - off[1]) % 4

    gather_up = [parents(order) for order in GATHER_ORDER]
    reduce_up = [parents(order) for order in REDUCE_ORDER]

    def sem_id(color, off, half):
        return (color * 32 + index_of(off)) * 2 + (half or 0)

    def gather(color, off):
        slot = gather_slot(off)
        if off != (0, 0, 0):
            for _, axis, step, half in gather_up[color][off]:
                start, rows = span(color, half)
                view = x_all.at[slot, pl.ds(start, rows), :]
                remote(view, view, ag_send, ag_recv.at[sem_id(color, off, half)], neighbour(axis, -step)).wait_recv()
        for kid, axis, step, half in children(GATHER_ORDER[color], off):
            start, rows = span(color, half)
            view = x_all.at[slot, pl.ds(start, rows), :]
            remote(view, view, ag_send, ag_recv.at[sem_id(color, kid, half)], neighbour(axis, step)).start()

    def products(ox, oy):
        to_x, to_y = (x + 4 - ox) % 4, (y + 4 - oy) % 4
        units = jnp.concatenate([g_all[zl * 4 + to_x], g_all[(1 - zl) * 4 + to_x]], axis=0)
        base = index_of((ox, oy, 0))

        def tile(i, carry):
            lines = pl.ds(pl.multiple_of(to_y * 1024 + i * 256, 256), 256)
            got = lax.dot_general(w_buf[lines, :], units, (((1,), (1,)), ((), ())),
                                  preferred_element_type=jnp.float32)
            into = pl.ds(pl.multiple_of(i * 256, 256), 256)
            part[base, into, :] = got[:, :128]
            part[base + 1, into, :] = got[:, 128:]
            return carry

        lax.fori_loop(0, 4, tile, 0)

    def reduce(color, off):
        at = index_of(off)
        for kid, axis, step, half in children(REDUCE_ORDER[color], off):
            start, rows = span(color, half)
            src = landed.at[index_of(kid), pl.ds(start, rows), :]
            remote(src, src, rs_send, rs_recv.at[sem_id(color, kid, half)], neighbour(axis, step)).wait_recv()
            part[at, pl.ds(start, rows), :] = part[at, pl.ds(start, rows), :] + landed[index_of(kid), pl.ds(start, rows), :]
        if off != (0, 0, 0):
            for _, axis, step, half in reduce_up[color][off]:
                start, rows = span(color, half)
                remote(part.at[at, pl.ds(start, rows), :], landed.at[at, pl.ds(start, rows), :], rs_send,
                       rs_recv.at[sem_id(color, off, half)], neighbour(axis, -step)).start()

    staged = []

    def weights(color, oy):
        start, rows = ROWS[color]
        from_y = (y + 4 - oy) % 4
        slot = len(staged) % 2
        if len(staged) >= 2:
            staged[-2].wait()
        left = jnp.concatenate([x_all[i * 4 + from_y, pl.ds(start, rows), :] for i in range(8)], axis=1)
        got = jnp.dot(left, g_all[...].reshape(1024, 896), preferred_element_type=jnp.float32)
        stage[slot, pl.ds(0, rows), :] = got.astype(jnp.bfloat16)
        copy = pltpu.make_async_copy(
            stage.at[slot, pl.ds(0, rows), :],
            gw_ref.at[pl.ds(pl.multiple_of(from_y * 1024 + start, 128), rows), :], out_sem.at[slot])
        copy.start()
        staged.append(copy)

    fetched = False

    def fetch():
        for i in range(4):
            slot = core * 4 + i
            pltpu.make_async_copy(g_all.at[slot], g_all.at[slot], g_recv.at[slot]).wait()
            remote(g_all.at[slot], g_all.at[slot], h_send.at[i], g_recv.at[slot],
                   {"gx": gx, "gy": zh * 2 + 1 - core, "gz": y}).start()
        for i in range(4):
            slot = (1 - core) * 4 + i
            pltpu.make_async_copy(g_all.at[slot], g_all.at[slot], g_recv.at[slot]).wait()
        w_copy.wait()

    for kind, first, off in program:
        if kind == "ag":
            gather(first, off)
        elif kind == "rs":
            reduce(first, off)
        else:
            if not fetched:
                fetch()
                fetched = True
            if kind == "pp":
                products(first, off)
            else:
                weights(first, off)

    gi_ref[...] = part[0].T.astype(jnp.bfloat16)

    for copy in staged[-2:]:
        copy.wait()
    for half in range(2):
        for far in range(2):
            to_x, to_y = zh * 4 + 2 * core + half, far * 2 + zl
            src = go_ref.at[:, pl.ds(half * 896, 896)]

            @pl.when(jnp.logical_not(jnp.logical_and(to_x == gx, to_y == gy)))
            def _():
                remote(src, g_all.at[gx], g_send.at[2 * half + far], g_recv.at[gx],
                       {"gx": to_x, "gy": to_y, "gz": y}).wait_send()
    for i in range(4):
        slot = core * 4 + i
        remote(g_all.at[slot], g_all.at[slot], h_send.at[i], g_recv.at[slot],
               {"gx": gx, "gy": zh * 2 + 1 - core, "gz": y}).wait_send()
    sent = x_all.at[pl.ds(0, 31)]
    pltpu.make_async_copy(sent, sent, ag_send).wait()
    sent = part.at[pl.ds(0, 31)]
    pltpu.make_async_copy(sent, sent, rs_send).wait()


def local(x_saved, grad_out, weight):
    program, _ = plan(4)
    vmem = pl.BlockSpec(memory_space=pltpu.VMEM)
    anywhere = pl.BlockSpec(memory_space=pl.ANY)
    return pl.pallas_call(
        functools.partial(body, program=program),
        out_shape=(jax.ShapeDtypeStruct((128, 1024), jnp.bfloat16),
                   jax.ShapeDtypeStruct((4096, 896), jnp.bfloat16)),
        in_specs=[vmem, vmem, anywhere],
        out_specs=(vmem, anywhere),
        scratch_shapes=[
            pltpu.VMEM((4096, 896), jnp.bfloat16),
            pltpu.VMEM((32, 1024, 128), jnp.bfloat16),
            pltpu.VMEM((8, 128, 896), jnp.bfloat16),
            pltpu.VMEM((32, 1024, 128), jnp.float32),
            pltpu.VMEM((32, 1024, 128), jnp.float32),
            pltpu.VMEM((2, 384, 896), jnp.bfloat16),
            pltpu.SemaphoreType.DMA,
            pltpu.SemaphoreType.DMA,
            pltpu.SemaphoreType.DMA((192,)),
            pltpu.SemaphoreType.DMA,
            pltpu.SemaphoreType.DMA((192,)),
            pltpu.SemaphoreType.DMA((4,)),
            pltpu.SemaphoreType.DMA((8,)),
            pltpu.SemaphoreType.DMA((4,)),
            pltpu.SemaphoreType.DMA((2,)),
        ],
        compiler_params=pltpu.CompilerParams(has_side_effects=True, vmem_limit_bytes=67043328),
    )(x_saved, grad_out, weight)


def solution(mesh):
    return jax.shard_map(
        local,
        mesh=mesh,
        in_specs=(P("gx", ("gy", "gz")), P("gx", ("gz", "gy")), P("gy", ("gz", "gx"))),
        out_specs=(P("gx", ("gy", "gz")), P("gy", ("gz", "gx"))),
        check_vma=False,
    )
```

time: 387 us -> 156 us (0.40)
  waiting for transfers between devices: 288 us -> 0 us
  Pallas kernels: 0 us -> 147 us
  blocking collectives: 46.1 us -> 0 us
  matrix products: 26 us -> 0 us
  between operations: 13.8 us -> 0.64 us
    reduce_scatter x1 -> x0, waiting for transfers between devices: 189 us -> none  [body(): lax.psum_scatter(terms, ('gx', 'gz'), scatter_dimension=0, tiled=True)]
    pallas_call x0 -> x1, Pallas kernels: none -> 147 us  [local(): pl.pallas_call(functools.partial(body, program=program), out_shape=(jax.S...]
    all_gather x3 -> x0, waiting for transfers between devices: 97.9 us -> none  [the longest x1 43.9 us: body(): lax.all_gather(inputs_block, 'gx', axis=0, tiled=True)]
    all_to_all x1 -> x0, blocking collectives: 46.1 us -> none  [body(): lax.all_to_all(grad_block, 'gx', split_axis=1, concat_axis=0, tiled=True)]
    dot_general x2 -> x0, matrix products: 26 us -> none  [the longest x1 14.2 us: body(): jnp.einsum('td,tc->dc', lax.all_gather(inputs_block, 'gx', axis=0, tiled=...]
    unnamed x5 -> x2, local copies, waits for them, and re-layouts: 2 us -> 8.38 us
    transpose x1 -> x0, local copies, waits for them, and re-layouts: 6.11 us -> none  [body(): jnp.einsum('atc,bkc->abtk', grad_split, weight_split, preferred_element_t...]
  transfers between devices with their start and end apart: 4 -> 0, of which waited for: 4 -> 0; matrix products, arithmetic and copies ran while one was open for 10% -> 0% of each run, Pallas kernels for 0% -> 0%
where the time goes in v1:
time: 156 us
  Pallas kernels  147 us (94%)
  local copies, waits for them, and re-layouts  8.38 us (5%)
    pallas_call x1, Pallas kernels, local(): pl.pallas_call(functools.partial(body, program=program), out_shape=(jax.S...  147 us
    unnamed x2, local copies, waits for them, and re-layouts  8.38 us

profile of v1, /device:TPU:0, one launch (start us, length us, event | category | flops | bytes accessed | tf_op | source)
XLA Modules:
  0.0 155.8 jit_solution(11307929214069858304)
XLA Ops:
  0.6 146.8 %shard_map.50 = (bf16[128,1024]{1,0:T(8,128)(2,1)}, bf16[4096,896]{1,0:T(8,128)(2,1)}) custom-call(bf16[128,1024]{1,0:T(8,128)(2,1)} %x_ref.1, bf16[128,1792]{1,0:T(8,128)(2,1)} %go_ref.1, bf16[4096,896]{1,0:T(8,128)(2,1)} %w_ref.1), custom_call_target="tpu_custom_call" | custom-call | tf_op jit(solution)/shard_map/pallas_call | solution.py:300
  147.4 1.7 %copy.7 = bf16[128,1024]{1,0:T(8,128)(2,1)} copy(bf16[128,1024]{1,0:T(8,128)(2,1)} %get-tuple-element.4) | data formatting | bytes 524288
  149.1 6.7 %copy.8 = bf16[4096,896]{1,0:T(8,128)(2,1)} copy(bf16[4096,896]{1,0:T(8,128)(2,1)} %get-tuple-element.5) | data formatting | bytes 14680064

commit v2 on v1

v2 whole, which is shorter than its diff:
```python
import functools

import jax
import jax.numpy as jnp
from jax import lax
from jax.experimental import pallas as pl
from jax.experimental.pallas import tpu as pltpu
from jax.sharding import PartitionSpec as P

SIZE = {"x": 4, "y": 4, "z": 2}
AXES = ("x", "y", "z")
ROWS = ((0, 256), (256, 384), (640, 384))
GATHER_ORDER = (("x", "y", "z"), ("y", "z", "x"), ("z", "x", "y"))
REDUCE_ORDER = (("y", "x", "z"), ("x", "z", "y"), ("z", "y", "x"))
OFFSETS = tuple((a, b, c) for a in range(4) for b in range(4) for c in range(2))


def index_of(off):
    return (off[0] * 4 + off[1]) * 2 + off[2]


def children(order, off):
    at = dict(zip(AXES, off))
    last = max([i for i in range(3) if at[order[i]]], default=-1)
    found = []

    def child(axis, value):
        moved = dict(at)
        moved[axis] = value
        return tuple(moved[a] for a in AXES)

    if last >= 0 and SIZE[order[last]] == 4:
        axis = order[last]
        if at[axis] == 1:
            found.append((child(axis, 2), axis, 1, 0))
        if at[axis] == 3:
            found.append((child(axis, 2), axis, -1, 1))
    for i in range(last + 1, 3):
        axis = order[i]
        found.append((child(axis, 1), axis, 1, None))
        if SIZE[axis] == 4:
            found.append((child(axis, 3), axis, -1, None))
    return found


def parents(order):
    found = {}
    for off in OFFSETS:
        for kid, axis, step, half in children(order, off):
            found.setdefault(kid, []).append((off, axis, step, half))
    return found


def span(color, half):
    start, rows = ROWS[color]
    if half is None:
        return start, rows
    return start + half * (rows // 2), rows // 2


def plan(rate=46500.0, delay=1.8):
    free = {("x", 1): 0.0, ("x", -1): 0.0, ("y", 1): 0.0, ("y", -1): 0.0, ("z", 1): 0.0, ("h", 1): 0.0}
    arrive = {}
    piece = 128 * 896

    def move(key, link, now, nbytes):
        free[link] = max(free[link], now) + nbytes / rate
        arrive[key] = free[link] + delay

    def send(kind, color, kid, axis, step, half, now, nbytes):
        move((kind, color, kid, half), (axis, step if SIZE[axis] == 4 else 1), now, nbytes)

    tasks = []
    reduce_up = [parents(order) for order in REDUCE_ORDER]
    gather_up = [parents(order) for order in GATHER_ORDER]
    for color in range(3):
        for off in OFFSETS:
            tasks.append(("ag", color, off))
            tasks.append(("rs", color, off))
    for oy in range(4):
        for color in range(3):
            tasks.append(("gw", color, oy))
    for ox in range(4):
        for oy in range(4):
            tasks.append(("pp", ox, oy))
        for kind in ("g1", "g2", "g3", "gh"):
            tasks.append((kind, ox, 0))
    distance = (0, 1, 2, 1)
    done = {}
    now = 2.5
    arrive[("g1", 0)] = 3.0
    move(("g1", 1), ("x", 1), now, piece)
    move(("g1", 3), ("x", -1), now, piece)
    move(("g1", 2), ("x", 1), now, 2 * piece)
    program = []

    def ready(task):
        kind, first, off = task
        if kind == "ag":
            if off == (0, 0, 0):
                return 2.5
            need = [("ag", first, off, half) for _, _, _, half in gather_up[first][off]]
        elif kind == "rs":
            if ("pp", off[0], off[1]) not in done:
                return None
            need = [("rs", first, kid, half) for kid, _, _, half in children(REDUCE_ORDER[first], off)]
        elif kind == "pp":
            if ("gh", first, 0) not in done or ("g3", first, 0) not in done:
                return None
            need = []
        elif kind == "gw":
            if any(("ag", first, (a, off, c)) not in done for a in range(4) for c in range(2)):
                return None
            if any(("gh", a, 0) not in done for a in range(4)):
                return None
            need = []
        else:
            need = [(kind, first)]
        if any(n not in arrive for n in need):
            return None
        return max([arrive[n] for n in need], default=0.0)

    def rank(task, at):
        kind = task[0]
        if kind[0] == "g" and kind != "gw":
            return (0, at, str(task))
        if kind in ("ag", "rs"):
            return (1, at, str(task))
        if kind == "pp":
            return (2, -(distance[task[1]] + distance[task[2]]), str(task))
        return (3, 0.0, str(task))

    cost = {"ag": 0.05, "rs": 0.4, "pp": 0.9, "gw": 1.2, "g1": 0.05, "g2": 0.05, "g3": 0.05, "gh": 0.05}
    while tasks:
        options = [(ready(t), t) for t in tasks]
        options = [(r, t) for r, t in options if r is not None]
        open_now = [(r, t) for r, t in options if r <= now]
        if not open_now:
            now = min(r for r, _ in options)
            continue
        _, task = min(open_now, key=lambda item: rank(item[1], item[0]))
        tasks.remove(task)
        program.append(task)
        kind, first, off = task
        now += cost[kind]
        done[task] = now
        if kind == "g1":
            move(("g2", first), ("h", 1), now, piece)
        if kind == "g2":
            move(("g3", first), ("z", 1), now, piece)
        if kind == "g3":
            arrive[("gh", first)] = now + 2.0
        if kind == "ag":
            for kid, axis, step, half in children(GATHER_ORDER[first], off):
                send("ag", first, kid, axis, step, half, now, span(first, half)[1] * 256)
        if kind == "rs" and off != (0, 0, 0):
            for _, axis, step, half in reduce_up[first][off]:
                send("rs", first, off, axis, -step, half, now, coded(first, half)[1] * 256)
    return program, now


CHUNK = 64
BLOCK = 1024 + 3 * 16
LAND = 1024 + 3 * 32
TOP = 125.0
LN2 = 0.6931471805599453


def coded(color, half):
    start, rows = ROWS[color]
    base = start + 16 * color
    if half is None:
        return base, rows + 16
    return base + half * (rows // 2), rows // 2 + 16


def body(x_ref, go_ref, w_ref, gi_ref, gw_ref, w_buf, x_all, g_all, part, code, landed, stage,
         w_sem, ag_send, ag_recv, rs_send, rs_recv, x_send, p_send, g_recv, out_sem, *, program):
    gx, gy, y = lax.axis_index("gx"), lax.axis_index("gy"), lax.axis_index("gz")
    zl, x = gx // 4, gx % 4
    zh, core = gy // 2, gy % 2
    primary = core == x // 2
    outer = zh == zl

    def neighbour(axis, step):
        if axis == "x":
            return {"gx": zl * 4 + (x + step + 4) % 4, "gy": gy, "gz": y}
        if axis == "y":
            return {"gx": gx, "gy": gy, "gz": (y + step + 4) % 4}
        return {"gx": (1 - zl) * 4 + x, "gy": gy, "gz": y}

    pair = neighbour("z", 1)
    across = {"gx": (1 - zl) * 4 + x, "gy": (1 - zh) * 2 + core, "gz": y}
    sibling = {"gx": gx, "gy": zh * 2 + 1 - core, "gz": y}

    def pick(a, b):
        if isinstance(a, dict):
            return {k: jnp.where(outer, a[k], b[k]) for k in a}
        return jnp.where(outer, a, b)

    def remote(src, dst, send_sem, recv_sem, device):
        return pltpu.make_async_remote_copy(
            src_ref=src, dst_ref=dst, send_sem=send_sem, recv_sem=recv_sem,
            device_id=device, device_id_type=pl.DeviceIdType.MESH)

    greeted = [neighbour("x", 1), neighbour("x", -1), neighbour("x", 2), neighbour("y", 1), neighbour("y", -1),
               pair, across, sibling]
    barrier = pltpu.get_barrier_semaphore()
    for device in greeted:
        pl.semaphore_signal(barrier, inc=1, device_id=device, device_id_type=pl.DeviceIdType.MESH)

    w_copy = pltpu.make_async_copy(w_ref, w_buf, w_sem)
    w_copy.start()
    x_all[gx * 4 + y] = x_ref[...].T
    pl.semaphore_wait(barrier, len(greeted))

    def first_hop(half, start):
        to_x = 2 * core + half
        src = go_ref.at[:, pl.ds(half * 896, 896)]
        dst = g_all.at[pick(zl * 4 + x, 8 + x)]

        if start:
            @pl.when(to_x == x)
            def _():
                pltpu.make_async_copy(src, dst, g_recv.at[x]).start()

        @pl.when(to_x != x)
        def _():
            copy = remote(src, dst, x_send.at[half], g_recv.at[x], {"gx": zl * 4 + to_x, "gy": gy, "gz": y})
            if start:
                copy.start()
            else:
                copy.wait_send()

    first_hop(0, True)
    first_hop(1, True)

    def landed_g(slot, sem):
        pltpu.make_async_copy(g_all.at[slot], g_all.at[slot], g_recv.at[sem]).wait()

    def passes(kind, ox):
        fx = (x + 4 - ox) % 4
        mine, other = zl * 4 + fx, (1 - zl) * 4 + fx
        if kind == "g1":
            at = pick(mine, 8 + fx)
            return at, fx, [
                remote(g_all.at[at], g_all.at[pick(8 + fx, mine)], p_send.at[ox * 4], g_recv.at[4 + fx], across),
                remote(g_all.at[at], g_all.at[mine], p_send.at[ox * 4 + 1], g_recv.at[pick(12 + mine, 8 + fx)],
                       pick(sibling, pair))]
        if kind == "g2":
            at = pick(8 + fx, other)
            return at, 4 + fx, [
                remote(g_all.at[at], g_all.at[other], p_send.at[ox * 4 + 2], g_recv.at[pick(8 + fx, 12 + other)],
                       pick(pair, sibling))]
        at = pick(other, mine)
        return at, 8 + fx, [
            remote(g_all.at[at], g_all.at[at], p_send.at[ox * 4 + 3], g_recv.at[12 + at], sibling)]

    def spread(kind, ox):
        if kind == "gh":
            @pl.when(jnp.logical_not(primary))
            def _():
                fx = (x + 4 - ox) % 4
                landed_g(fx, 12 + fx)
                landed_g(4 + fx, 16 + fx)
            return

        @pl.when(primary)
        def _():
            at, sem, copies = passes(kind, ox)
            landed_g(at, sem)
            for copy in copies:
                copy.start()

    def gather_slot(off):
        return ((zl + off[2]) % 2 * 4 + (x + 4 - off[0]) % 4) * 4 + (y + 4 - off[1]) % 4

    gather_up = [parents(order) for order in GATHER_ORDER]
    reduce_up = [parents(order) for order in REDUCE_ORDER]

    def sem_id(color, off, half):
        return (color * 32 + index_of(off)) * 2 + (half or 0)

    def gather(color, off):
        slot = gather_slot(off)
        if off != (0, 0, 0):
            for _, axis, step, half in gather_up[color][off]:
                start, rows = span(color, half)
                view = x_all.at[slot, pl.ds(start, rows), :]
                remote(view, view, ag_send, ag_recv.at[sem_id(color, off, half)], neighbour(axis, -step)).wait_recv()
        for kid, axis, step, half in children(GATHER_ORDER[color], off):
            start, rows = span(color, half)
            view = x_all.at[slot, pl.ds(start, rows), :]
            remote(view, view, ag_send, ag_recv.at[sem_id(color, kid, half)], neighbour(axis, step)).start()

    def products(ox, oy):
        to_x, to_y = (x + 4 - ox) % 4, (y + 4 - oy) % 4
        units = jnp.concatenate([g_all[zl * 4 + to_x], g_all[(1 - zl) * 4 + to_x]], axis=0)
        base = index_of((ox, oy, 0))

        def tile(i, carry):
            lines = pl.ds(pl.multiple_of(to_y * 1024 + i * 256, 256), 256)
            got = lax.dot_general(w_buf[lines, :], units, (((1,), (1,)), ((), ())),
                                  preferred_element_type=jnp.float32)
            into = pl.ds(pl.multiple_of(i * 256, 256), 256)
            part[base, into, :] = got[:, :128]
            part[base + 1, into, :] = got[:, 128:]
            return carry

        lax.fori_loop(0, 4, tile, 0)

    def code_view(off, color, half):
        start, rows = coded(color, half)
        return code.at[pl.ds(index_of(off) * BLOCK + start, rows), :]

    def land_view(off, color, half):
        start, rows = coded(color, half)
        return landed.at[pl.ds(index_of(off) * LAND + start + 16 * color + 16 * (half or 0), rows), :]

    def add_child(color, at, kid, half):
        start, rows = ROWS[color]
        from_row = index_of(kid) * LAND + start + 32 * color + 16 * (half or 0)
        unit = landed[pl.ds(from_row + rows // 2, 16), :][0:1].astype(jnp.float32) * (1.0 / (2 * TOP * LN2))
        for side in (0, 1) if half is None else (half,):
            def chunk(i, carry):
                src = pl.ds(pl.multiple_of(from_row + side * (rows // 2 + 16) + i * CHUNK, 16), CHUNK)
                dst = pl.ds(pl.multiple_of(start + side * (rows // 2) + i * CHUNK, CHUNK), CHUNK)
                got = landed[src, :].astype(jnp.float32)
                size = (jnp.log(jnp.abs(got)) + TOP * LN2) * unit
                part[at, dst, :] = part[at, dst, :] + jnp.where(got < 0, -size, size)
                return carry

            lax.fori_loop(0, rows // 2 // CHUNK, chunk, 0)

    def encode(color, at):
        start, rows = ROWS[color]

        def largest(i, carry):
            view = part[at, pl.ds(pl.multiple_of(start + i * CHUNK, CHUNK), CHUNK), :]
            return jnp.maximum(carry, jnp.max(jnp.abs(view).reshape(CHUNK // 8, 8, 128), axis=0))

        most = lax.fori_loop(0, rows // CHUNK, largest, jnp.zeros((8, 128), jnp.float32))
        most = jnp.max(most, axis=0, keepdims=True)
        scale = jnp.maximum(most * 1.01, 1e-35).astype(jnp.bfloat16)
        unit = (2 * TOP) / scale.astype(jnp.float32)
        to_row = at * BLOCK + start + 16 * color
        code[pl.ds(to_row + rows // 2, 16), :] = jnp.broadcast_to(scale, (16, 128))
        for side in range(2):
            def chunk(i, carry):
                src = pl.ds(pl.multiple_of(start + side * (rows // 2) + i * CHUNK, CHUNK), CHUNK)
                dst = pl.ds(pl.multiple_of(to_row + side * (rows // 2 + 16) + i * CHUNK, 16), CHUNK)
                value = part[at, src, :]
                size = lax.exp2(jnp.abs(value) * unit - TOP)
                code[dst, :] = jnp.where(value < 0, -size, size).astype(jnp.bfloat16)
                return carry

            lax.fori_loop(0, rows // 2 // CHUNK, chunk, 0)

    def reduce(color, off):
        at = index_of(off)
        for kid, axis, step, half in children(REDUCE_ORDER[color], off):
            src = land_view(kid, color, half)
            remote(src, src, rs_send, rs_recv.at[sem_id(color, kid, half)], neighbour(axis, step)).wait_recv()
            add_child(color, at, kid, half)
        if off != (0, 0, 0):
            encode(color, at)
            for _, axis, step, half in reduce_up[color][off]:
                remote(code_view(off, color, half), land_view(off, color, half), rs_send,
                       rs_recv.at[sem_id(color, off, half)], neighbour(axis, -step)).start()

    staged = []

    def weights(color, oy):
        start, rows = ROWS[color]
        from_y = (y + 4 - oy) % 4
        slot = len(staged) % 2
        if len(staged) >= 2:
            staged[-2].wait()
        left = jnp.concatenate([x_all[i * 4 + from_y, pl.ds(start, rows), :] for i in range(8)], axis=1)
        got = jnp.dot(left, g_all[pl.ds(0, 8)].reshape(1024, 896), preferred_element_type=jnp.float32)
        stage[slot, pl.ds(0, rows), :] = got.astype(jnp.bfloat16)
        copy = pltpu.make_async_copy(
            stage.at[slot, pl.ds(0, rows), :],
            gw_ref.at[pl.ds(pl.multiple_of(from_y * 1024 + start, 128), rows), :], out_sem.at[slot])
        copy.start()
        staged.append(copy)

    has_w = False
    for kind, first, off in program:
        if kind == "ag":
            gather(first, off)
        elif kind == "rs":
            reduce(first, off)
        elif kind == "gw":
            weights(first, off)
        elif kind == "pp":
            if not has_w:
                w_copy.wait()
                has_w = True
            products(first, off)
        else:
            spread(kind, first)

    gi_ref[...] = part[0].T.astype(jnp.bfloat16)

    for copy in staged[-2:]:
        copy.wait()
    first_hop(0, False)
    first_hop(1, False)

    @pl.when(primary)
    def _():
        for kind in ("g1", "g2", "g3"):
            for ox in range(4):
                for copy in passes(kind, ox)[2]:
                    copy.wait_send()

    sent = x_all.at[pl.ds(0, 31)]
    pltpu.make_async_copy(sent, sent, ag_send).wait()
    rows = sum(coded(color, half)[1] for color in range(3) for ups in reduce_up[color].values() for _, _, _, half in ups)
    sent = code.at[pl.ds(0, rows), :]
    pltpu.make_async_copy(sent, sent, rs_send).wait()


def local(x_saved, grad_out, weight):
    program, _ = plan()
    vmem = pl.BlockSpec(memory_space=pltpu.VMEM)
    anywhere = pl.BlockSpec(memory_space=pl.ANY)
    return pl.pallas_call(
        functools.partial(body, program=program),
        out_shape=(pltpu.VMEM((128, 1024), jnp.bfloat16),
                   jax.ShapeDtypeStruct((4096, 896), jnp.bfloat16)),
        in_specs=[vmem, vmem, anywhere],
        out_specs=(vmem, anywhere),
        scratch_shapes=[
            pltpu.VMEM((4096, 896), jnp.bfloat16),
            pltpu.VMEM((32, 1024, 128), jnp.bfloat16),
            pltpu.VMEM((12, 128, 896), jnp.bfloat16),
            pltpu.VMEM((32, 1024, 128), jnp.float32),
            pltpu.VMEM((32 * BLOCK, 128), jnp.bfloat16),
            pltpu.VMEM((32 * LAND, 128), jnp.bfloat16),
            pltpu.VMEM((2, 384, 896), jnp.bfloat16),
            pltpu.SemaphoreType.DMA,
            pltpu.SemaphoreType.DMA,
            pltpu.SemaphoreType.DMA((192,)),
            pltpu.SemaphoreType.DMA,
            pltpu.SemaphoreType.DMA((192,)),
            pltpu.SemaphoreType.DMA((2,)),
            pltpu.SemaphoreType.DMA((16,)),
            pltpu.SemaphoreType.DMA((20,)),
            pltpu.SemaphoreType.DMA((2,)),
        ],
        compiler_params=pltpu.CompilerParams(collective_id=0, has_side_effects=True, vmem_limit_bytes=63 * 1024 * 1024),
    )(x_saved, grad_out, weight)


def solution(mesh):
    return jax.shard_map(
        local,
        mesh=mesh,
        in_specs=(P("gx", ("gy", "gz")), P("gx", ("gz", "gy")), P("gy", ("gz", "gx"))),
        out_specs=(P("gx", ("gy", "gz")), P("gy", ("gz", "gx"))),
        check_vma=False,
    )
```

time: 156 us -> 117 us (0.75)
  Pallas kernels: 147 us -> 108 us
    pallas_call x1, Pallas kernels: 147 us -> 108 us  [local(): pl.pallas_call(functools.partial(body, program=program), out_shape=(pltpu...]
where the time goes in v2:
time: 117 us; the launch traced here: 116 us
  Pallas kernels  108 us (92%)
  local copies, waits for them, and re-layouts  7.42 us (6%)
    pallas_call x1, Pallas kernels, local(): pl.pallas_call(functools.partial(body, program=program), out_shape=(pltpu...  108 us
    unnamed x2, local copies, waits for them, and re-layouts  7.42 us

profile of v2, /device:TPU:0, one launch (start us, length us, event | category | flops | bytes accessed | tf_op | source)
XLA Modules:
  0.0 116.0 jit_solution(16592836233304192263)
XLA Ops:
  0.6 107.9 %shard_map.50 = (bf16[128,1024]{1,0:T(8,128)(2,1)S(1)}, bf16[4096,896]{1,0:T(8,128)(2,1)}) custom-call(bf16[128,1024]{1,0:T(8,128)(2,1)} %x_ref.1, bf16[128,1792]{1,0:T(8,128)(2,1)} %go_ref.1, bf16[4096,896]{1,0:T(8,128)(2,1)} %w_ref.1), custom_call_target="tpu_custom_call" | custom-call | tf_op jit(solution)/shard_map/pallas_call | solution.py:429
  108.6 0.7 copy.7
  109.3 6.7 %copy.8 = bf16[4096,896]{1,0:T(8,128)(2,1)} copy(bf16[4096,896]{1,0:T(8,128)(2,1)} %get-tuple-element.7) | data formatting | bytes 14680064

commit v3 on v2

--- a/solution.py
+++ b/solution.py
@@ -58,21 +58,22 @@
     return start + half * (rows // 2), rows // 2
 
 
-def plan(rate=46500.0, delay=1.8):
-    free = {("x", 1): 0.0, ("x", -1): 0.0, ("y", 1): 0.0, ("y", -1): 0.0, ("z", 1): 0.0, ("h", 1): 0.0}
-    arrive = {}
-    piece = 128 * 896
-
-    def move(key, link, now, nbytes):
-        free[link] = max(free[link], now) + nbytes / rate
-        arrive[key] = free[link] + delay
-
-    def send(kind, color, kid, axis, step, half, now, nbytes):
-        move((kind, color, kid, half), (axis, step if SIZE[axis] == 4 else 1), now, nbytes)
-
+ORDER = (
+    0, 128, 208, 64, 216, 209, 130, 48, 4, 210, 68, 176, 2, 224, 232, 144, 76, 178, 116, 211, 134, 225, 146, 70,
+    233, 124, 205, 66, 217, 16, 204, 12, 7, 50, 84, 226, 72, 156, 234, 160, 227, 162, 223, 222, 142, 78, 182,
+    235, 107, 43, 175, 218, 8, 206, 28, 219, 215, 105, 132, 126, 213, 173, 171, 174, 20, 75, 74, 32, 221, 112,
+    118, 18, 165, 140, 86, 39, 109, 220, 101, 229, 169, 167, 150, 92, 35, 214, 60, 111, 73, 230, 207, 181, 6,
+    82, 155, 14, 31, 34, 172, 11, 27, 121, 91, 52, 159, 187, 190, 77, 228, 123, 188, 47, 37, 15, 180, 114, 87,
+    80, 100, 161, 185, 164, 41, 30, 231, 36, 163, 103, 59, 122, 212, 44, 153, 189, 22, 69, 191, 149, 23, 119,
+    117, 38, 120, 127, 19, 54, 138, 151, 89, 158, 98, 145, 203, 51, 96, 148, 57, 95, 99, 194, 71, 46, 136, 139,
+    137, 62, 168, 40, 183, 21, 115, 166, 45, 94, 193, 201, 25, 63, 79, 83, 55, 90, 10, 179, 152, 108, 88, 197,
+    157, 143, 85, 56, 110, 97, 102, 135, 93, 3, 147, 125, 106, 186, 61, 133, 202, 9, 184, 33, 29, 24, 141, 42,
+    53, 154, 67, 177, 196, 81, 131, 192, 104, 58, 113, 170, 5, 17, 26, 13, 49, 195, 198, 199, 200, 129, 65, 1
+)
+
+
+def plan():
     tasks = []
-    reduce_up = [parents(order) for order in REDUCE_ORDER]
-    gather_up = [parents(order) for order in GATHER_ORDER]
     for color in range(3):
         for off in OFFSETS:
             tasks.append(("ag", color, off))
@@ -85,78 +86,7 @@
             tasks.append(("pp", ox, oy))
         for kind in ("g1", "g2", "g3", "gh"):
             tasks.append((kind, ox, 0))
-    distance = (0, 1, 2, 1)
-    done = {}
-    now = 2.5
-    arrive[("g1", 0)] = 3.0
-    move(("g1", 1), ("x", 1), now, piece)
-    move(("g1", 3), ("x", -1), now, piece)
-    move(("g1", 2), ("x", 1), now, 2 * piece)
-    program = []
-
-    def ready(task):
-        kind, first, off = task
-        if kind == "ag":
-            if off == (0, 0, 0):
-                return 2.5
-            need = [("ag", first, off, half) for _, _, _, half in gather_up[first][off]]
-        elif kind == "rs":
-            if ("pp", off[0], off[1]) not in done:
-                return None
-            need = [("rs", first, kid, half) for kid, _, _, half in children(REDUCE_ORDER[first], off)]
-        elif kind == "pp":
-            if ("gh", first, 0) not in done or ("g3", first, 0) not in done:
-                return None
-            need = []
-        elif kind == "gw":
-            if any(("ag", first, (a, off, c)) not in done for a in range(4) for c in range(2)):
-                return None
-            if any(("gh", a, 0) not in done for a in range(4)):
-                return None
-            need = []
-        else:
-            need = [(kind, first)]
-        if any(n not in arrive for n in need):
-            return None
-        return max([arrive[n] for n in need], default=0.0)
-
-    def rank(task, at):
-        kind = task[0]
-        if kind[0] == "g" and kind != "gw":
-            return (0, at, str(task))
-        if kind in ("ag", "rs"):
-            return (1, at, str(task))
-        if kind == "pp":
-            return (2, -(distance[task[1]] + distance[task[2]]), str(task))
-        return (3, 0.0, str(task))
-
-    cost = {"ag": 0.05, "rs": 0.4, "pp": 0.9, "gw": 1.2, "g1": 0.05, "g2": 0.05, "g3": 0.05, "gh": 0.05}
-    while tasks:
-        options = [(ready(t), t) for t in tasks]
-        options = [(r, t) for r, t in options if r is not None]
-        open_now = [(r, t) for r, t in options if r <= now]
-        if not open_now:
-            now = min(r for r, _ in options)
-            continue
-        _, task = min(open_now, key=lambda item: rank(item[1], item[0]))
-        tasks.remove(task)
-        program.append(task)
-        kind, first, off = task
-        now += cost[kind]
-        done[task] = now
-        if kind == "g1":
-            move(("g2", first), ("h", 1), now, piece)
-        if kind == "g2":
-            move(("g3", first), ("z", 1), now, piece)
-        if kind == "g3":
-            arrive[("gh", first)] = now + 2.0
-        if kind == "ag":
-            for kid, axis, step, half in children(GATHER_ORDER[first], off):
-                send("ag", first, kid, axis, step, half, now, span(first, half)[1] * 256)
-        if kind == "rs" and off != (0, 0, 0):
-            for _, axis, step, half in reduce_up[first][off]:
-                send("rs", first, off, axis, -step, half, now, coded(first, half)[1] * 256)
-    return program, now
+    return [tasks[i] for i in ORDER]
 
 
 CHUNK = 64
@@ -174,8 +104,8 @@
     return base + half * (rows // 2), rows // 2 + 16
 
 
-def body(x_ref, go_ref, w_ref, gi_ref, gw_ref, w_buf, x_all, g_all, part, code, landed, stage,
-         w_sem, ag_send, ag_recv, rs_send, rs_recv, x_send, p_send, g_recv, out_sem, *, program):
+def body(x_ref, go_ref, w_ref, gi_ref, gw_ref, w_buf, x_all, g_all, part, code, landed,
+         w_sem, ag_send, ag_recv, rs_send, rs_recv, x_send, p_send, g_recv, *, program):
     gx, gy, y = lax.axis_index("gx"), lax.axis_index("gy"), lax.axis_index("gz")
     zl, x = gx // 4, gx % 4
     zh, core = gy // 2, gy % 2
@@ -368,22 +298,12 @@
                 remote(code_view(off, color, half), land_view(off, color, half), rs_send,
                        rs_recv.at[sem_id(color, off, half)], neighbour(axis, -step)).start()
 
-    staged = []
-
     def weights(color, oy):
         start, rows = ROWS[color]
         from_y = (y + 4 - oy) % 4
-        slot = len(staged) % 2
-        if len(staged) >= 2:
-            staged[-2].wait()
         left = jnp.concatenate([x_all[i * 4 + from_y, pl.ds(start, rows), :] for i in range(8)], axis=1)
         got = jnp.dot(left, g_all[pl.ds(0, 8)].reshape(1024, 896), preferred_element_type=jnp.float32)
-        stage[slot, pl.ds(0, rows), :] = got.astype(jnp.bfloat16)
-        copy = pltpu.make_async_copy(
-            stage.at[slot, pl.ds(0, rows), :],
-            gw_ref.at[pl.ds(pl.multiple_of(from_y * 1024 + start, 128), rows), :], out_sem.at[slot])
-        copy.start()
-        staged.append(copy)
+        gw_ref[pl.ds(pl.multiple_of(from_y * 1024 + start, 128), rows), :] = got.astype(jnp.bfloat16)
 
     has_w = False
     for kind, first, off in program:
@@ -403,8 +323,6 @@
 
     gi_ref[...] = part[0].T.astype(jnp.bfloat16)
 
-    for copy in staged[-2:]:
-        copy.wait()
     first_hop(0, False)
     first_hop(1, False)
 
@@ -423,15 +341,15 @@
 
 
 def local(x_saved, grad_out, weight):
-    program, _ = plan()
+    program = plan()
     vmem = pl.BlockSpec(memory_space=pltpu.VMEM)
     anywhere = pl.BlockSpec(memory_space=pl.ANY)
     return pl.pallas_call(
         functools.partial(body, program=program),
         out_shape=(pltpu.VMEM((128, 1024), jnp.bfloat16),
-                   jax.ShapeDtypeStruct((4096, 896), jnp.bfloat16)),
+                   pltpu.VMEM((4096, 896), jnp.bfloat16)),
         in_specs=[vmem, vmem, anywhere],
-        out_specs=(vmem, anywhere),
+        out_specs=(vmem, vmem),
         scratch_shapes=[
             pltpu.VMEM((4096, 896), jnp.bfloat16),
             pltpu.VMEM((32, 1024, 128), jnp.bfloat16),
@@ -439,7 +357,6 @@
             pltpu.VMEM((32, 1024, 128), jnp.float32),
             pltpu.VMEM((32 * BLOCK, 128), jnp.bfloat16),
             pltpu.VMEM((32 * LAND, 128), jnp.bfloat16),
-            pltpu.VMEM((2, 384, 896), jnp.bfloat16),
             pltpu.SemaphoreType.DMA,
             pltpu.SemaphoreType.DMA,
             pltpu.SemaphoreType.DMA((192,)),
@@ -448,9 +365,8 @@
             pltpu.SemaphoreType.DMA((2,)),
             pltpu.SemaphoreType.DMA((16,)),
             pltpu.SemaphoreType.DMA((20,)),
-            pltpu.SemaphoreType.DMA((2,)),
         ],
-        compiler_params=pltpu.CompilerParams(collective_id=0, has_side_effects=True, vmem_limit_bytes=63 * 1024 * 1024),
+        compiler_params=pltpu.CompilerParams(collective_id=0, has_side_effects=True, vmem_limit_bytes=53 * 1024 * 1024),
     )(x_saved, grad_out, weight)
 
 

time: 117 us -> 106 us (0.906)
  Pallas kernels: 108 us -> 102 us
  local copies, waits for them, and re-layouts: 7.42 us -> 3.75 us
    pallas_call x1, Pallas kernels: 108 us -> 102 us  [local(): pl.pallas_call(functools.partial(body, program=program), out_shape=(pltpu...]
    unnamed x2, local copies, waits for them, and re-layouts: 7.42 us -> 3.75 us
where the time goes in v3:
time: 106 us
  Pallas kernels  102 us (96%)
  local copies, waits for them, and re-layouts  3.75 us (4%)
    pallas_call x1, Pallas kernels, local(): pl.pallas_call(functools.partial(body, program=program), out_shape=(pltpu...  102 us
    unnamed x2, local copies, waits for them, and re-layouts  3.75 us

profile of v3, /device:TPU:0, one launch (start us, length us, event | category | flops | bytes accessed | tf_op | source)
XLA Modules:
  0.0 105.9 jit_solution(11877026230194362573)
XLA Ops:
  0.6 101.5 %shard_map.50 = (bf16[128,1024]{1,0:T(8,128)(2,1)S(1)}, bf16[4096,896]{1,0:T(8,128)(2,1)S(1)}) custom-call(bf16[128,1024]{1,0:T(8,128)(2,1)} %x_ref.1, bf16[128,1792]{1,0:T(8,128)(2,1)} %go_ref.1, bf16[4096,896]{1,0:T(8,128)(2,1)} %w_ref.1), custom_call_target="tpu_custom_call" | custom-call | tf_op jit(solution)/shard_map/pallas_call | solution.py:347
  102.2 0.7 copy.7
  102.9 3.0 %copy.8 = bf16[4096,896]{1,0:T(8,128)(2,1)} copy(bf16[4096,896]{1,0:T(8,128)(2,1)S(1)} %get-tuple-element.3) | data formatting | bytes 14680064

commit v4 on v3

--- a/solution.py
+++ b/solution.py
@@ -11,7 +11,7 @@
 AXES = ("x", "y", "z")
 ROWS = ((0, 256), (256, 384), (640, 384))
 GATHER_ORDER = (("x", "y", "z"), ("y", "z", "x"), ("z", "x", "y"))
-REDUCE_ORDER = (("y", "x", "z"), ("x", "z", "y"), ("z", "y", "x"))
+REDUCE_ORDER = GATHER_ORDER
 OFFSETS = tuple((a, b, c) for a in range(4) for b in range(4) for c in range(2))
 
 
@@ -59,16 +59,16 @@
 
 
 ORDER = (
-    0, 128, 208, 64, 216, 209, 130, 48, 4, 210, 68, 176, 2, 224, 232, 144, 76, 178, 116, 211, 134, 225, 146, 70,
-    233, 124, 205, 66, 217, 16, 204, 12, 7, 50, 84, 226, 72, 156, 234, 160, 227, 162, 223, 222, 142, 78, 182,
-    235, 107, 43, 175, 218, 8, 206, 28, 219, 215, 105, 132, 126, 213, 173, 171, 174, 20, 75, 74, 32, 221, 112,
-    118, 18, 165, 140, 86, 39, 109, 220, 101, 229, 169, 167, 150, 92, 35, 214, 60, 111, 73, 230, 207, 181, 6,
-    82, 155, 14, 31, 34, 172, 11, 27, 121, 91, 52, 159, 187, 190, 77, 228, 123, 188, 47, 37, 15, 180, 114, 87,
-    80, 100, 161, 185, 164, 41, 30, 231, 36, 163, 103, 59, 122, 212, 44, 153, 189, 22, 69, 191, 149, 23, 119,
-    117, 38, 120, 127, 19, 54, 138, 151, 89, 158, 98, 145, 203, 51, 96, 148, 57, 95, 99, 194, 71, 46, 136, 139,
-    137, 62, 168, 40, 183, 21, 115, 166, 45, 94, 193, 201, 25, 63, 79, 83, 55, 90, 10, 179, 152, 108, 88, 197,
-    157, 143, 85, 56, 110, 97, 102, 135, 93, 3, 147, 125, 106, 186, 61, 133, 202, 9, 184, 33, 29, 24, 141, 42,
-    53, 154, 67, 177, 196, 81, 131, 192, 104, 58, 113, 170, 5, 17, 26, 13, 49, 195, 198, 199, 200, 129, 65, 1
+    0, 128, 208, 64, 209, 216, 130, 232, 48, 176, 68, 76, 224, 16, 210, 60, 144, 211, 178, 225, 70, 205, 206,
+    217, 146, 72, 137, 28, 116, 180, 132, 207, 233, 226, 156, 190, 158, 66, 80, 218, 227, 20, 182, 52, 139, 222,
+    74, 107, 32, 204, 84, 124, 171, 219, 140, 214, 43, 24, 223, 142, 30, 12, 169, 134, 221, 56, 143, 78, 188,
+    234, 103, 27, 213, 120, 101, 162, 34, 235, 86, 220, 44, 91, 111, 148, 136, 100, 99, 2, 126, 4, 135, 118, 23,
+    109, 230, 175, 82, 41, 153, 152, 36, 47, 160, 59, 212, 114, 8, 123, 94, 112, 167, 54, 88, 150, 92, 187, 229,
+    165, 87, 22, 25, 14, 83, 228, 138, 215, 105, 35, 155, 18, 40, 173, 174, 39, 185, 122, 90, 231, 46, 7, 6,
+    191, 63, 57, 119, 11, 194, 166, 62, 172, 50, 104, 75, 164, 15, 127, 121, 95, 151, 31, 115, 159, 125, 184,
+    10, 89, 189, 97, 38, 203, 42, 157, 183, 163, 61, 26, 21, 192, 45, 98, 110, 181, 96, 161, 85, 193, 37, 102,
+    168, 58, 55, 79, 9, 93, 106, 51, 108, 117, 198, 73, 149, 71, 154, 147, 29, 141, 196, 179, 202, 81, 177, 53,
+    5, 195, 19, 33, 67, 199, 170, 186, 133, 77, 145, 131, 113, 13, 69, 197, 3, 17, 49, 200, 201, 65, 129, 1
 )
 
 

time: 106 us -> 103 us (0.972)
  Pallas kernels: 102 us -> 98.9 us
    pallas_call x1, Pallas kernels: 102 us -> 98.9 us  [local(): pl.pallas_call(functools.partial(body, program=program), out_shape=(pltpu...]
where the time goes in v4:
time: 103 us
  Pallas kernels  98.9 us (96%)
  local copies, waits for them, and re-layouts  3.75 us (4%)
    pallas_call x1, Pallas kernels, local(): pl.pallas_call(functools.partial(body, program=program), out_shape=(pltpu...  98.9 us
    unnamed x2, local copies, waits for them, and re-layouts  3.75 us

profile of v4, /device:TPU:0, one launch (start us, length us, event | category | flops | bytes accessed | tf_op | source)
XLA Modules:
  0.0 103.3 jit_solution(1487487919725367294)
XLA Ops:
  0.6 98.9 %shard_map.50 = (bf16[128,1024]{1,0:T(8,128)(2,1)S(1)}, bf16[4096,896]{1,0:T(8,128)(2,1)S(1)}) custom-call(bf16[128,1024]{1,0:T(8,128)(2,1)} %x_ref.1, bf16[128,1792]{1,0:T(8,128)(2,1)} %go_ref.1, bf16[4096,896]{1,0:T(8,128)(2,1)} %w_ref.1), custom_call_target="tpu_custom_call" | custom-call | tf_op jit(solution)/shard_map/pallas_call | solution.py:347
  99.5 0.7 copy.7
  100.2 3.0 %copy.8 = bf16[4096,896]{1,0:T(8,128)(2,1)} copy(bf16[4096,896]{1,0:T(8,128)(2,1)S(1)} %get-tuple-element.3) | data formatting | bytes 14680064
